TPU v7x, 128 devices: a whole 4x4x4 slice. The times are simulated.
128 devices in a mesh: grp: 16 (over x, z_hi, core), seq: 8 (over y, z_lo).
Axes of the slice: x: 4, y: 4, z: 4 (z_hi: 2, z_lo: 2; z = z_hi * 2 + z_lo), core: 2. Of those that a mesh axis runs over, the one named last changes fastest.
Arguments:
- lengths: int32 [32], replicated, may hold values from 64 to 2048, as said below
- group_of: int32 [32], replicated, may hold values from 0 to 15, as said below
- query_pre: bfloat16 [32768, 8192], P(('grp', 'seq')), may hold values from -170 to 170
- key_pre: bfloat16 [32768, 1024], P(('grp', 'seq')), may hold values from -7 to 7
- value_pre: bfloat16 [32768, 1024], P(('grp', 'seq')), may hold values from -4 to 4
- query_new: bfloat16 [32, 8192], P(None, 'seq'), may hold values from -170 to 170
- key_new: bfloat16 [32, 1024], P(None, 'seq'), may hold values from -4 to 4
- value_new: bfloat16 [32, 1024], P(None, 'seq'), may hold values from -4 to 4
- hidden_new: bfloat16 [32, 8192], P(None, 'grp'), may hold values from -3 to 3
- out_weight: bfloat16 [8192, 8192], P('seq', 'grp'), may hold values from -0.0625 to 0.0625
- norm_gain: bfloat16 [8192], P('grp'), may hold values from 0.099609375 to 1.8984375
- gate_weight: bfloat16 [8192, 16384], P('grp', 'seq'), may hold values from -0.0625 to 0.0625
- up_weight: bfloat16 [8192, 16384], P('grp', 'seq'), may hold values from -0.0625 to 0.0625
- down_weight: bfloat16 [16384, 8192], P('seq', 'grp'), may hold values from -0.046875 to 0.046875
Outputs:
- prefill_attention: bfloat16 [32768, 8192], P(('grp', 'seq'))
- decode_hidden: bfloat16 [32, 8192], P(None, ('grp', 'seq'))
Inputs may be any that keep to these rules, and one draw needn't show every extreme that they name: Two requests have length exactly 2048 and are alone in their groups; the others have lengths from 64 to 512; the lengths in one group sum to at most 2048. `group_of`: every group holds at least one request and at most three.
All inputs are finite; a program needn't handle non-finite values.
Results may differ from a plain program's by a relative error of at most 0.0095.
Values may be sent and summed in bfloat16 or wider, within the bound.
A program may use at most 320 MiB of HBM per device.

v0:
```python
import math
import jax
import jax.numpy as jnp
from jax import lax
from jax.sharding import PartitionSpec as P

D = 8192
H = 64
KVH = 8
HD = 128
NEGATIVE = -1e30


def request_starts(lengths, group_of):
    index = jnp.arange(lengths.shape[0], dtype=jnp.int32)
    same = group_of[None, :] == group_of[:, None]
    before = index[None, :] < index[:, None]
    return jnp.sum(jnp.where(same & before, lengths[None, :], 0), axis=1)


def slot_owner(group_idx, starts, lengths, group_of, count):
    slots = jnp.arange(count, dtype=jnp.int32)
    inside = (
        (group_of[None, :] == group_idx)
        & (slots[:, None] >= starts[None, :])
        & (slots[:, None] < (starts + lengths)[None, :])
    )
    labels = jnp.arange(lengths.shape[0], dtype=jnp.int32) + 1
    return jnp.sum(jnp.where(inside, labels[None, :], 0), axis=1) - 1


def block_scores(queries, keys, owner_rows, owner_cols, row_first):
    count_q = queries.shape[0]
    count_k = keys.shape[0]
    kv_heads = keys.shape[1] // HD
    grouped = queries.shape[1] // (HD * kv_heads)
    query_heads = queries.reshape(count_q, kv_heads, grouped, HD)
    key_heads = keys.reshape(count_k, kv_heads, HD)
    scores = jnp.einsum(
        "qkgd,tkd->kgqt", query_heads, key_heads, preferred_element_type=jnp.float32
    ) * (1.0 / math.sqrt(HD))
    rows = row_first + jnp.arange(count_q, dtype=jnp.int32)
    columns = jnp.arange(count_k, dtype=jnp.int32)
    allowed = (
        (owner_rows[:, None] == owner_cols[None, :])
        & (owner_rows[:, None] >= 0)
        & (columns[None, :] <= rows[:, None])
    )
    return (jnp.where(allowed[None, None], scores, NEGATIVE), allowed)


def online_step(carry, queries, keys, values, owner_rows, owner_cols, row_first):
    top, total, accum = carry
    count = keys.shape[0]
    kv_heads = keys.shape[1] // HD
    scores, allowed = block_scores(queries, keys, owner_rows, owner_cols, row_first)
    new_top = jnp.maximum(top, jnp.max(scores, axis=-1))
    weights = jnp.where(allowed[None, None], jnp.exp(scores - new_top[..., None]), 0.0)
    total = jnp.sum(weights, axis=-1)
    value_heads = values.reshape(count, kv_heads, HD)
    mixed = jnp.einsum(
        "kgqt,tkd->qkgd",
        weights.astype(jnp.bfloat16),
        value_heads,
        preferred_element_type=jnp.float32,
    )
    accum = mixed
    return (new_top, total, accum)


def empty_carry(rows, kv_heads, grouped):
    init_top = jnp.full((kv_heads, grouped, rows), NEGATIVE, jnp.float32)
    init_total = jnp.zeros((kv_heads, grouped, rows), jnp.float32)
    init_acc = jnp.zeros((rows, kv_heads, grouped, HD), jnp.float32)
    return (init_top, init_total, init_acc)


def finish(mixed, total, owner_rows):
    live = owner_rows >= 0
    denom = jnp.where(live[None, None, :], total, 1.0)
    result = mixed / jnp.transpose(denom, (2, 0, 1))[..., None]
    result = jnp.where(live[:, None, None, None], result, 0.0)
    return result.reshape(result.shape[0], -1).astype(jnp.bfloat16)


def decode_attend(query_new, key_new, value_new, cache_keys, cache_values, owners):
    requests = query_new.shape[0]
    kv_heads = cache_keys.shape[1] // HD
    grouped = query_new.shape[1] // (HD * kv_heads)
    query_heads = query_new.reshape(requests, kv_heads, grouped, HD)
    key_heads = cache_keys.reshape(cache_keys.shape[0], kv_heads, HD)
    value_heads = cache_values.reshape(cache_values.shape[0], kv_heads, HD)
    scale = 1.0 / math.sqrt(HD)
    scores = (
        jnp.einsum("rkgd,tkd->rkgt", query_heads, key_heads, preferred_element_type=jnp.float32)
        * scale
    )
    own = (
        jnp.einsum(
            "rkgd,rkd->rkg",
            query_heads,
            key_new.reshape(requests, kv_heads, HD),
            preferred_element_type=jnp.float32,
        )
        * scale
    )
    match = owners[None, :] == jnp.arange(requests, dtype=jnp.int32)[:, None]
    scores = jnp.where(match[:, None, None, :], scores, NEGATIVE)
    top = jnp.maximum(jnp.max(scores, axis=-1), own)
    weights = jnp.where(match[:, None, None, :], jnp.exp(scores - top[..., None]), 0.0)
    own_weight = jnp.exp(own - top)
    total = jnp.sum(weights, axis=-1) + own_weight
    mixed = jnp.einsum(
        "rkgt,tkd->rkgd",
        weights.astype(jnp.bfloat16),
        value_heads,
        preferred_element_type=jnp.float32,
    )
    own_value = value_new.reshape(requests, kv_heads, 1, HD).astype(jnp.float32)
    mixed = mixed + own_weight.astype(jnp.bfloat16).astype(jnp.float32)[..., None] * own_value
    return (mixed / total[..., None]).reshape(requests, -1).astype(jnp.bfloat16)


def shards(
    lengths,
    group_of,
    query_pre,
    key_pre,
    value_pre,
    query_new,
    key_new,
    value_new,
    hidden_new,
    out_weight,
    norm_gain,
    gate_weight,
    up_weight,
    down_weight,
):
    seq_count = lax.axis_size("seq")
    seq_index = lax.axis_index("seq")
    group_idx = lax.axis_index("grp")
    tokens_dev = query_pre.shape[0]
    group_slots = tokens_dev * seq_count
    starts = request_starts(lengths, group_of)
    owners = slot_owner(group_idx, starts, lengths, group_of, group_slots)
    cache_keys, cache_values = (
        lax.all_to_all(key_pre, "seq", split_axis=1, concat_axis=0, tiled=True),
        lax.all_to_all(value_pre, "seq", split_axis=1, concat_axis=0, tiled=True),
    )
    my_first = seq_index * tokens_dev
    my_last = my_first + tokens_dev - 1
    owner_rows = lax.dynamic_slice_in_dim(owners, my_first, tokens_dev, 0)
    any_live = jnp.any(owner_rows >= 0)
    grouped = H // KVH
    piece_keys = lax.all_gather(key_pre, "seq", axis=0, tiled=True)
    piece_values = lax.all_gather(value_pre, "seq", axis=0, tiled=True)
    needed = (jnp.int32(0) <= my_last) & any_live

    def attend(state):
        return online_step(state, query_pre, piece_keys, piece_values, owner_rows, owners, my_first)

    def keep(state):
        return state

    top, total, accum = lax.cond(needed, attend, keep, empty_carry(tokens_dev, KVH, grouped))
    prefill_attention = finish(accum, total, owner_rows)
    attended = decode_attend(query_new, key_new, value_new, cache_keys, cache_values, owners)
    mine = group_of == group_idx
    attended = jnp.where(mine[:, None], attended, jnp.zeros_like(attended))
    decode_att = lax.psum(attended, "grp").astype(jnp.float32).astype(jnp.bfloat16)
    proj_part = jnp.dot(decode_att, out_weight, preferred_element_type=jnp.float32)
    projected = lax.psum(proj_part, "seq")
    resid = hidden_new.astype(jnp.float32) + projected
    squares = lax.psum(jnp.sum(resid * resid, axis=-1), "grp")
    normed = (
        resid * lax.rsqrt(squares / D + 1e-05)[:, None] * norm_gain.astype(jnp.float32)[None, :]
    ).astype(jnp.bfloat16)
    gate_part = jnp.dot(normed, gate_weight, preferred_element_type=jnp.float32)
    upper_part = jnp.dot(normed, up_weight, preferred_element_type=jnp.float32)
    gate, upper = lax.psum((gate_part, upper_part), "grp")
    hidden = (jax.nn.silu(gate) * upper).astype(jnp.bfloat16)
    down_part = jnp.dot(hidden, down_weight, preferred_element_type=jnp.float32)
    down_share = lax.psum_scatter(down_part, "seq", scatter_dimension=1, tiled=True)
    width = down_share.shape[1]
    resid_share = lax.dynamic_slice_in_dim(resid, seq_index * width, width, 1)
    decode_hidden = (resid_share + down_share).astype(jnp.bfloat16)
    return (prefill_attention, decode_hidden)


def solution(mesh):
    return jax.shard_map(
        shards,
        mesh=mesh,
        in_specs=(
            P(),
            P(),
            P(("grp", "seq"), None),
            P(("grp", "seq"), None),
            P(("grp", "seq"), None),
            P(None, "seq"),
            P(None, "seq"),
            P(None, "seq"),
            P(None, "grp"),
            P("seq", "grp"),
            P("grp"),
            P("grp", "seq"),
            P("grp", "seq"),
            P("seq", "grp"),
        ),
        out_specs=(P(("grp", "seq"), None), P(None, ("grp", "seq"))),
        check_vma=False,
    )
```

profile of v0, /device:TPU:23, one launch (start us, length us, event | category | flops | bytes accessed | tf_op | source)
XLA Modules:
  0.0 828.9 jit_solution(12726307764702582196)
XLA Ops:
  7.2 2.1 copy_bitcast_fusion.2
  9.3 5.6 all-to-all-start
  14.9 0.7 broadcast_compare_fusion.2
  15.5 0.9 select_reduce_fusion.1
  16.5 0.7 add.73
  17.1 0.8 copy.74
  18.0 1.9 copy_bitcast_fusion.1
  19.9 0.8 fusion.36
  20.8 0.2 select_reduce_fusion
  20.9 0.1 copy.60
  21.0 0.7 convert_element_type.57
  21.8 5.5 all-to-all-start.1
  27.3 0.5 fusion.46
  27.9 1.3 copy-done.1
  29.2 0.5 fusion.21
  29.7 3.8 all-to-all-done.1
  33.5 2.1 fusion.25
  35.6 0.7 bitcast_select_fusion.1
  36.4 124.9 %all-reduce.5.cloned.1.call-done = bf16[32,1024]{1,0:T(8,128)(2,1)} async-done(((bf16[32,1024]{1,0:T(8,128)(2,1)}), bf16[32,1024]{1,0:T(8,128)(2,1)}) %all-reduce.5.cloned.1.call-update) | async-done | bytes 65552 | tf_op jit(solution)/shard_map/psum | solution.py:171
  161.3 2.2 fusion.47
  163.5 0.0 all-reduce.9.cloned.1.call-start
  163.6 70.2 %all-reduce.7.cloned.1.call-done = f32[32,512]{1,0:T(8,128)} async-done(((f32[32,512]{1,0:T(8,128)}), f32[32,512]{1,0:T(8,128)}) %all-reduce.7.cloned.1.call-update) | async-done | bytes 65552 | tf_op jit(solution)/shard_map/psum | solution.py:173
  233.7 1.0 multiply_reduce_fusion
  234.7 33.4 %psum.37 = f32[32]{0:T(128)S(1)} all-reduce(f32[32]{0:T(128)S(1)} %get-tuple-element.28), channel_id=1, replica_groups=mesh['grp'=16,'seq'=8] {'grp'}, use_global_device_ids=true, to_apply=%region_12.13 | all-reduce | flops 32 | bytes 256 | tf_op jit(solution)/shard_map/psum | solution.py:175
  268.1 1.2 fusion.44
  269.3 2.8 fusion.43
  272.2 139.1 %all-reduce.9.cloned.1.call-done = (f32[32,2048]{1,0:T(8,128)}, f32[32,2048]{1,0:T(8,128)}) async-done(((f32[32,2048]{1,0:T(8,128)}, f32[32,2048]{1,0:T(8,128)}), (f32[32,2048]{1,0:T(8,128)}, f32[32,2048]{1,0:T(8,128)})) %all-reduce.9.cloned.1.call-update) | async-done | bytes 524304 | tf_op jit(solution)/shard_map/psum | solution.py:181
  411.3 3.4 convolution_bitcast_fusion
  414.8 0.5 all-gather.3.cloned.1.call-update
  415.4 0.5 all-gather.5.cloned.1.call-update
  415.9 1.2 fusion.45
  417.8 28.3 %reduce-scatter.4.cloned.1.call-done = f32[64,32]{1,0:T(8,128)} async-done(((f32[512,32]{1,0:T(8,128)}), f32[64,32]{1,0:T(8,128)}) %reduce-scatter.4.cloned.1.call-update) | async-done | bytes 8208
  446.1 0.8 copy.66
  446.9 0.7 add_convert_fusion
  447.6 98.0 %all-gather.3.cloned.1.call-done = bf16[2048,1024]{1,0:T(8,128)(2,1)} async-done(((bf16[256,1024]{1,0:T(8,128)(2,1)}), bf16[2048,1024]{1,0:T(8,128)(2,1)}) %all-gather.3.cloned.1.call-update) | async-done | bytes 4194320 | tf_op jit(solution)/shard_map/all_gather | solution.py:156
  545.6 93.8 %all-gather.5.cloned.1.call-done = bf16[2048,1024]{1,0:T(8,128)(2,1)} async-done(((bf16[256,1024]{1,0:T(8,128)(2,1)}), bf16[2048,1024]{1,0:T(8,128)(2,1)}) %all-gather.5.cloned.1.call-update) | async-done | bytes 4194320 | tf_op jit(solution)/shard_map/all_gather | solution.py:157
  639.4 163.5 %conditional.1 = (f32[8,8,256]{2,1,0:T(8,128)}, f32[256,8,8,128]{3,0,2,1:T(8,128)}) conditional(s32[]{:T(128)} %convert_element_type.50, () %tuple.16, (s32[256]{0:T(256)S(1)}, s32[2048]{0:T(1024)S(1)}, s32[]{:T(128)}, bf16[2048,1024]{1,0:T(8,128)(2,1)}, bf16[256,8192]{1,0:T(8,128)(2,1)}, /*index=5*/bf16[2048,1024]{1,0:T(8,128)(2,1)}) %tuple.17), branch_computations={%region_3.4_spmd, %region_4.7_spmd} | conditional | flops 17618157568 | bytes 468070976 | solution.py:166
  639.5 0.7 fusion.15
  640.2 5.4 copy.67
  645.6 3.2 copy.68
  648.8 52.7 %fusion = (f32[8,8,256]{2,1,0:T(8,128)S(1)}, f32[8,2048,256,8]{2,1,3,0:T(8,128)}) fusion(pred[256,2048]{0,1:T(8,128)(4,1)S(1)} %fusion.15, bf16[256,8,8,128]{3,2,1,0:T(8,128)(2,1)} %bitcast.116, bf16[2048,8,128,1]{2,1,0,3:T(8,128)(2,1)} %bitcast.117), kind=kOutput, calls=%fused_computation.2 | convolution fusion | flops 8690581504 | bytes 143196160 | tf_op jit(solution)/shard_map/cond/branch_1_fun/qkgd,tkd->kgqt/dot_general | solution.py:39
  701.5 5.3 copy.69
  706.8 54.3 %fusion.10 = f32[256,8,8,128]{3,0,2,1:T(8,128)} fusion(bf16[2048,8,128,1]{2,1,0,3:T(8,128)(2,1)} %bitcast.123, f32[8,2048,256,8]{2,1,3,0:T(8,128)} %get-tuple-element.34, f32[8,8,256]{2,1,0:T(8,128)S(1)} %broadcast_maximum_fusion, pred[256,2048]{0,1:T(8,128)(4,1)S(1)} %fusion.15), kind=kOutput, calls=%fused_computation.11 | convolution fusion | flops 8757706752 | bytes 147390464 | tf_op jit(solution)/shard_map/cond/branch_1_fun/kgqt,tkd->qkgd/dot_general | solution.py:61
  761.1 41.9 %fusion.2 = f32[8,8,256]{2,1,0:T(8,128)} fusion(f32[8,2048,256,8]{2,1,3,0:T(8,128)} %get-tuple-element.34, f32[8,8,256]{2,1,0:T(8,128)S(1)} %broadcast_maximum_fusion, pred[256,2048]{0,1:T(8,128)(4,1)S(1)} %fusion.15), kind=kLoop, calls=%fused_computation.4 | loop fusion | flops 167755776 | bytes 134873088 | tf_op jit(solution)/shard_map/cond/branch_1_fun/reduce_sum | solution.py:59
  803.0 0.8 select_bitcast_fusion
  803.8 5.4 select_convert_fusion
  809.2 2.7 copy.51
  811.9 10.2 %copy.100 = bf16[32,8,64,128]{3,1,2,0:T(8,128)(2,1)} copy(bf16[32,8,64,128]{3,2,1,0:T(8,128)(2,1)S(1)} %bitcast.118) | data formatting | bytes 8388608
  (34 shorter events, 0.4 us)
Async XLA Ops:
  7.2 261.0 %copy-start = (bf16[512,2048]{1,0:T(8,128)(2,1)S(1)}, bf16[512,2048]{1,0:T(8,128)(2,1)}, u32[]{:S(2)}) copy-start(bf16[512,2048]{1,0:T(8,128)(2,1)} %param.27) | copy-start | bytes 6291460
  7.2 20.1 %copy-start.3 = (bf16[32,1024]{1,0:T(8,128)(2,1)S(1)}, bf16[32,1024]{1,0:T(8,128)(2,1)}, u32[]{:S(2)}) copy-start(bf16[32,1024]{1,0:T(8,128)(2,1)} %param.21) | copy-start | bytes 196612
  9.3 12.5 %all-to-all-start = ((bf16[256,8,128]{2,0,1:T(8,128)(2,1)}), bf16[256,8,128]{2,0,1:T(8,128)(2,1)S(1)}, u32[]{:S(2)}, u32[]{:S(2)}) async-start(bf16[256,8,128]{2,0,1:T(8,128)(2,1)} %copy_bitcast_fusion.2), calls=%async_computation | async-start | bytes 1048576 | tf_op jit(solution)/shard_map/all_to_all | solution.py:148
  21.8 11.7 %all-to-all-start.1 = ((bf16[256,8,128]{2,0,1:T(8,128)(2,1)}), bf16[256,8,128]{2,0,1:T(8,128)(2,1)S(1)}, u32[]{:S(2)}, u32[]{:S(2)}) async-start(bf16[256,8,128]{2,0,1:T(8,128)(2,1)} %copy_bitcast_fusion.1), calls=%async_computation.1 | async-start | bytes 1048576 | tf_op jit(solution)/shard_map/all_to_all | solution.py:149
  27.3 134.0 %all-reduce.5.cloned.1.call-start = ((), (), s32[]{:S(2)}) async-start(), calls=%async_computation.5 | async-start | bytes 131072 | tf_op jit(solution)/shard_map/psum | solution.py:171
  27.8 1.3 copy-start.1
  27.9 135.7 %copy-start.6 = (bf16[512]{0:T(512)(128)(2,1)S(1)}, bf16[512]{0:T(512)(128)(2,1)}, u32[]{:S(2)}) copy-start(bf16[512]{0:T(512)(128)(2,1)} %param.26) | copy-start | bytes 3076
  27.9 205.9 %copy-start.4 = (bf16[32,512]{1,0:T(8,128)(2,1)S(1)}, bf16[32,512]{1,0:T(8,128)(2,1)}, u32[]{:S(2)}) copy-start(bf16[32,512]{1,0:T(8,128)(2,1)} %param.24) | copy-start | bytes 98308
  36.4 197.4 %all-reduce.7.cloned.1.call-start = ((), (), s32[]{:S(2)}) async-start(), calls=%async_computation.6 | async-start | bytes 131072 | tf_op jit(solution)/shard_map/psum | solution.py:173
  163.5 247.8 %all-reduce.9.cloned.1.call-start = ((), (), s32[]{:S(2)}) async-start(), calls=%async_computation.8 | async-start | bytes 1048576 | tf_op jit(solution)/shard_map/psum | solution.py:181
  272.2 173.9 %reduce-scatter.4.cloned.1.call-start = ((), (), s32[]{:S(2)}) async-start(), calls=%async_computation.7 | async-start | bytes 294912
  414.8 130.9 %all-gather.3.cloned.1.call-start = ((), (), s32[]{:S(2)}) async-start(), calls=%async_computation.3 | async-start | bytes 4718592 | tf_op jit(solution)/shard_map/all_gather | solution.py:156
  415.4 224.1 %all-gather.5.cloned.1.call-start = ((), (), s32[]{:S(2)}) async-start(), calls=%async_computation.4 | async-start | bytes 4718592 | tf_op jit(solution)/shard_map/all_gather | solution.py:157
  639.4 163.5 %copy-start.5 = (pred[256]{0:T(512)(128)(4,1)S(1)}, pred[256]{0:T(512)(128)(4,1)}, u32[]{:S(2)}) copy-start(pred[256]{0:T(512)(128)(4,1)} %get-tuple-element.31) | copy-start | bytes 772
  640.2 5.4 copy-start.2
Sparse Core Ops, SparseCore 0:
  36.5 124.7 all-reduce.4
  164.5 69.2 all-reduce.6
  272.3 138.9 all-reduce.8
  414.9 31.1 reduce-scatter.3
  447.6 98.0 all-gather.2
  547.1 92.2 all-gather.4
where the time goes:
time: 830 us; the launch traced here: 829 us
  waiting for transfers between devices  559 us (67%)
  matrix products  120 us (14%)
  other arithmetic  56.1 us (7%)
  local copies, waits for them, and re-layouts  33.9 us (4%)
  blocking collectives  33.4 us (4%)
  between operations  14.9 us (2%)
  starting transfers between devices  11.3 us (1%)
    psum x1, waiting for transfers between devices, shards(): gate, upper = lax.psum((gate_part, upper_part), 'grp')  139 us
    psum x1, waiting for transfers between devices, shards(): lax.psum(attended, 'grp').astype(jnp.float32).astype(jnp.bfloat16)  125 us
    all_gather x1, waiting for transfers between devices, shards(): piece_keys = lax.all_gather(key_pre, 'seq', axis=0, tiled=True)  98 us
    all_gather x1, waiting for transfers between devices, shards(): piece_values = lax.all_gather(value_pre, 'seq', axis=0, tiled=True)  93.8 us
    psum x1, waiting for transfers between devices, shards(): projected = lax.psum(proj_part, 'seq')  70.2 us
    dot_general x1, matrix products, online_step(): jnp.einsum('kgqt,tkd->qkgd', weights.astype(jnp.bfloat16), value_heads, p...  54.3 us
    dot_general x1, matrix products, block_scores(): jnp.einsum('qkgd,tkd->kgqt', query_heads, key_heads, preferred_element_ty...  52.7 us
    reduce_sum x1, other arithmetic, online_step(): total = jnp.sum(weights, axis=-1)  41.9 us
  transfers between devices with their start and end apart: 8, of which 7 were waited for; matrix products, arithmetic and copies ran while one was open for 1% of the time, Pallas kernels for 0%

commit v1 on v0

--- a/solution.py
+++ b/solution.py
@@ -154,7 +154,9 @@
     any_live = jnp.any(owner_rows >= 0)
     grouped = H // KVH
     piece_keys = lax.all_gather(key_pre, "seq", axis=0, tiled=True)
-    piece_values = lax.all_gather(value_pre, "seq", axis=0, tiled=True)
+    piece_values = jnp.concatenate(
+        lax.all_to_all(jnp.stack([value_pre] * lax.axis_size("seq")), "seq", 0, 0), axis=0
+    )
     needed = (jnp.int32(0) <= my_last) & any_live
 
     def attend(state):

time: 830 us -> 776 us (0.935)
  waiting for transfers between devices: 559 us -> 498 us
    all_gather x1 -> x0, waiting for transfers between devices: 93.8 us -> none  [shards(): piece_values = lax.all_gather(value_pre, 'seq', axis=0, tiled=True)]
    unnamed x7 -> x6, waiting for transfers between devices: 29.4 us -> 58.9 us
  transfers between devices with their start and end apart: 8 -> 8, of which waited for: 7 -> 6; matrix products, arithmetic and copies ran while one was open for 1% -> 2% of each run, Pallas kernels for 0% -> 0%
where the time goes in v1:
time: 776 us; the launch traced here: 774 us
  waiting for transfers between devices  498 us (64%)
  matrix products  120 us (15%)
  other arithmetic  56.1 us (7%)
  local copies, waits for them, and re-layouts  36.4 us (5%)
  blocking collectives  33.4 us (4%)
  starting transfers between devices  16 us (2%)
  between operations  14.6 us (2%)
    psum x1, waiting for transfers between devices, shards(): gate, upper = lax.psum((gate_part, upper_part), 'grp')  139 us
    psum x1, waiting for transfers between devices, shards(): lax.psum(attended, 'grp').astype(jnp.float32).astype(jnp.bfloat16)  125 us
    all_gather x1, waiting for transfers between devices, shards(): piece_keys = lax.all_gather(key_pre, 'seq', axis=0, tiled=True)  101 us
    psum x1, waiting for transfers between devices, shards(): projected = lax.psum(proj_part, 'seq')  70.2 us
    unnamed x6, waiting for transfers between devices  58.9 us
    dot_general x1, matrix products, online_step(): jnp.einsum('kgqt,tkd->qkgd', weights.astype(jnp.bfloat16), value_heads, p...  54.3 us
    dot_general x1, matrix products, block_scores(): jnp.einsum('qkgd,tkd->kgqt', query_heads, key_heads, preferred_element_ty...  52.7 us
    reduce_sum x1, other arithmetic, online_step(): total = jnp.sum(weights, axis=-1)  41.9 us
  transfers between devices with their start and end apart: 8, of which 6 were waited for; matrix products, arithmetic and copies ran while one was open for 2% of the time, Pallas kernels for 0%

profile of v1, /device:TPU:23, one launch (start us, length us, event | category | flops | bytes accessed | tf_op | source)
XLA Modules:
  0.0 774.3 jit_solution(4400843240223652202)
XLA Ops:
  7.2 2.1 copy_bitcast_fusion.2
  9.3 5.6 all-to-all-start.1
  14.9 0.7 broadcast_compare_fusion.2
  15.5 0.9 select_reduce_fusion.1
  16.5 0.7 add.73
  17.1 0.8 copy.74
  18.0 1.9 copy_bitcast_fusion.1
  19.9 0.8 fusion.36
  20.8 0.2 select_reduce_fusion
  20.9 0.1 copy.60
  21.0 0.7 convert_element_type.57
  21.8 5.5 all-to-all-start.2
  27.3 0.5 fusion.46
  27.9 1.3 copy-done.1
  29.2 0.5 fusion.21
  29.7 3.8 all-to-all-done.2
  33.5 2.1 fusion.25
  35.6 0.7 bitcast_select_fusion.1
  36.4 124.9 %all-reduce.5.cloned.1.call-done = bf16[32,1024]{1,0:T(8,128)(2,1)} async-done(((bf16[32,1024]{1,0:T(8,128)(2,1)}), bf16[32,1024]{1,0:T(8,128)(2,1)}) %all-reduce.5.cloned.1.call-update) | async-done | bytes 65552 | tf_op jit(solution)/shard_map/psum | solution.py:173
  161.3 2.2 fusion.47
  163.5 0.0 all-reduce.9.cloned.1.call-start
  163.6 70.2 %all-reduce.7.cloned.1.call-done = f32[32,512]{1,0:T(8,128)} async-done(((f32[32,512]{1,0:T(8,128)}), f32[32,512]{1,0:T(8,128)}) %all-reduce.7.cloned.1.call-update) | async-done | bytes 65552 | tf_op jit(solution)/shard_map/psum | solution.py:175
  233.7 1.0 multiply_reduce_fusion
  234.7 33.4 %psum.37 = f32[32]{0:T(128)S(1)} all-reduce(f32[32]{0:T(128)S(1)} %get-tuple-element.28), channel_id=1, replica_groups=mesh['grp'=16,'seq'=8] {'grp'}, use_global_device_ids=true, to_apply=%region_12.13 | all-reduce | flops 32 | bytes 256 | tf_op jit(solution)/shard_map/psum | solution.py:177
  268.1 1.2 fusion.44
  269.3 2.8 fusion.43
  272.2 139.1 %all-reduce.9.cloned.1.call-done = (f32[32,2048]{1,0:T(8,128)}, f32[32,2048]{1,0:T(8,128)}) async-done(((f32[32,2048]{1,0:T(8,128)}, f32[32,2048]{1,0:T(8,128)}), (f32[32,2048]{1,0:T(8,128)}, f32[32,2048]{1,0:T(8,128)})) %all-reduce.9.cloned.1.call-update) | async-done | bytes 524304 | tf_op jit(solution)/shard_map/psum | solution.py:183
  411.3 3.4 convolution_bitcast_fusion
  414.8 0.5 all-gather.2.cloned.1.call-update
  415.3 2.6 stack.2
  417.9 4.7 all-to-all-start
  422.6 1.2 fusion.45
  424.5 58.3 %reduce-scatter.4.cloned.1.call-done = f32[64,32]{1,0:T(8,128)} async-done(((f32[512,32]{1,0:T(8,128)}), f32[64,32]{1,0:T(8,128)}) %reduce-scatter.4.cloned.1.call-update) | async-done | bytes 8208
  482.8 0.8 copy.66
  483.6 0.7 add_convert_fusion
  484.3 100.9 %all-gather.2.cloned.1.call-done = bf16[2048,1024]{1,0:T(8,128)(2,1)} async-done(((bf16[256,1024]{1,0:T(8,128)(2,1)}), bf16[2048,1024]{1,0:T(8,128)(2,1)}) %all-gather.2.cloned.1.call-update) | async-done | bytes 4194320 | tf_op jit(solution)/shard_map/all_gather | solution.py:156
  585.2 163.5 %conditional.1 = (f32[8,8,256]{2,1,0:T(8,128)}, f32[256,8,8,128]{3,0,2,1:T(8,128)}) conditional(s32[]{:T(128)} %convert_element_type.50, () %tuple.16, (s32[256]{0:T(256)S(1)}, s32[2048]{0:T(1024)S(1)}, s32[]{:T(128)}, bf16[2048,1024]{1,0:T(8,128)(2,1)}, bf16[256,8192]{1,0:T(8,128)(2,1)}, /*index=5*/bf16[8,256,1024]{2,1,0:T(8,128)(2,1)}) %tuple.17), branch_computations={%region_3.4_spmd, %region_4.7_spmd} | conditional | flops 17618157568 | bytes 468070976 | solution.py:168
  585.2 0.7 fusion.15
  585.9 5.4 copy.67
  591.3 3.2 copy.68
  594.5 52.7 %fusion = (f32[8,8,256]{2,1,0:T(8,128)S(1)}, f32[8,2048,256,8]{2,1,3,0:T(8,128)}) fusion(pred[256,2048]{0,1:T(8,128)(4,1)S(1)} %fusion.15, bf16[256,8,8,128]{3,2,1,0:T(8,128)(2,1)} %bitcast.117, bf16[2048,8,128,1]{2,1,0,3:T(8,128)(2,1)} %bitcast.118), kind=kOutput, calls=%fused_computation.2 | convolution fusion | flops 8690581504 | bytes 143196160 | tf_op jit(solution)/shard_map/cond/branch_1_fun/qkgd,tkd->kgqt/dot_general | solution.py:39
  647.2 5.3 copy.69
  652.5 54.3 %fusion.10 = f32[256,8,8,128]{3,0,2,1:T(8,128)} fusion(bf16[2048,8,128,1]{2,1,0,3:T(8,128)(2,1)} %bitcast.123, f32[8,2048,256,8]{2,1,3,0:T(8,128)} %get-tuple-element.34, f32[8,8,256]{2,1,0:T(8,128)S(1)} %broadcast_maximum_fusion, pred[256,2048]{0,1:T(8,128)(4,1)S(1)} %fusion.15), kind=kOutput, calls=%fused_computation.11 | convolution fusion | flops 8757706752 | bytes 147390464 | tf_op jit(solution)/shard_map/cond/branch_1_fun/kgqt,tkd->qkgd/dot_general | solution.py:61
  706.8 41.9 %fusion.2 = f32[8,8,256]{2,1,0:T(8,128)} fusion(f32[8,2048,256,8]{2,1,3,0:T(8,128)} %get-tuple-element.34, f32[8,8,256]{2,1,0:T(8,128)S(1)} %broadcast_maximum_fusion, pred[256,2048]{0,1:T(8,128)(4,1)S(1)} %fusion.15), kind=kLoop, calls=%fused_computation.4 | loop fusion | flops 167755776 | bytes 134873088 | tf_op jit(solution)/shard_map/cond/branch_1_fun/reduce_sum | solution.py:59
  748.7 0.8 select_bitcast_fusion
  749.5 5.4 select_convert_fusion
  754.9 2.7 copy.51
  757.6 10.2 %copy.100 = bf16[32,8,64,128]{3,1,2,0:T(8,128)(2,1)} copy(bf16[32,8,64,128]{3,2,1,0:T(8,128)(2,1)S(1)} %bitcast.119) | data formatting | bytes 8388608
  (36 shorter events, 0.4 us)
Async XLA Ops:
  7.2 261.0 %copy-start = (bf16[512,2048]{1,0:T(8,128)(2,1)S(1)}, bf16[512,2048]{1,0:T(8,128)(2,1)}, u32[]{:S(2)}) copy-start(bf16[512,2048]{1,0:T(8,128)(2,1)} %param.27) | copy-start | bytes 6291460
  7.2 20.1 %copy-start.4 = (bf16[32,1024]{1,0:T(8,128)(2,1)S(1)}, bf16[32,1024]{1,0:T(8,128)(2,1)}, u32[]{:S(2)}) copy-start(bf16[32,1024]{1,0:T(8,128)(2,1)} %param.21) | copy-start | bytes 196612
  9.3 12.5 %all-to-all-start.1 = ((bf16[256,8,128]{2,0,1:T(8,128)(2,1)}), bf16[256,8,128]{2,0,1:T(8,128)(2,1)S(1)}, u32[]{:S(2)}, u32[]{:S(2)}) async-start(bf16[256,8,128]{2,0,1:T(8,128)(2,1)} %copy_bitcast_fusion.2), calls=%async_computation.1 | async-start | bytes 1048576 | tf_op jit(solution)/shard_map/all_to_all | solution.py:148
  21.8 11.7 %all-to-all-start.2 = ((bf16[256,8,128]{2,0,1:T(8,128)(2,1)}), bf16[256,8,128]{2,0,1:T(8,128)(2,1)S(1)}, u32[]{:S(2)}, u32[]{:S(2)}) async-start(bf16[256,8,128]{2,0,1:T(8,128)(2,1)} %copy_bitcast_fusion.1), calls=%async_computation.2 | async-start | bytes 1048576 | tf_op jit(solution)/shard_map/all_to_all | solution.py:149
  27.3 134.0 %all-reduce.5.cloned.1.call-start = ((), (), s32[]{:S(2)}) async-start(), calls=%async_computation.5 | async-start | bytes 131072 | tf_op jit(solution)/shard_map/psum | solution.py:173
  27.8 1.3 copy-start.1
  27.9 135.7 %copy-start.7 = (bf16[512]{0:T(512)(128)(2,1)S(1)}, bf16[512]{0:T(512)(128)(2,1)}, u32[]{:S(2)}) copy-start(bf16[512]{0:T(512)(128)(2,1)} %param.26) | copy-start | bytes 3076
  27.9 205.9 %copy-start.5 = (bf16[32,512]{1,0:T(8,128)(2,1)S(1)}, bf16[32,512]{1,0:T(8,128)(2,1)}, u32[]{:S(2)}) copy-start(bf16[32,512]{1,0:T(8,128)(2,1)} %param.24) | copy-start | bytes 98308
  36.4 197.4 %all-reduce.7.cloned.1.call-start = ((), (), s32[]{:S(2)}) async-start(), calls=%async_computation.6 | async-start | bytes 131072 | tf_op jit(solution)/shard_map/psum | solution.py:175
  163.5 247.8 %all-reduce.9.cloned.1.call-start = ((), (), s32[]{:S(2)}) async-start(), calls=%async_computation.8 | async-start | bytes 1048576 | tf_op jit(solution)/shard_map/psum | solution.py:183
  268.1 147.2 %copy-start.3 = (bf16[256,1024]{1,0:T(8,128)(2,1)S(1)}, bf16[256,1024]{1,0:T(8,128)(2,1)}, u32[]{:S(2)}) copy-start(bf16[256,1024]{1,0:T(8,128)(2,1)} %param.20) | copy-start | bytes 1572868
  272.2 210.6 %reduce-scatter.4.cloned.1.call-start = ((), (), s32[]{:S(2)}) async-start(), calls=%async_computation.7 | async-start | bytes 294912
  414.7 170.4 %all-gather.2.cloned.1.call-start = ((), (), s32[]{:S(2)}) async-start(), calls=%async_computation.4 | async-start | bytes 4718592 | tf_op jit(solution)/shard_map/all_gather | solution.py:156
  417.9 66.4 %all-to-all-start = ((bf16[8,256,1024]{2,1,0:T(8,128)(2,1)}), bf16[8,256,1024]{2,1,0:T(8,128)(2,1)}, u32[]{:S(2)}, u32[]{:S(2)}) async-start(bf16[8,256,1024]{2,1,0:T(8,128)(2,1)} %stack.2), calls=%async_computation | async-start | bytes 8388608 | tf_op jit(solution)/shard_map/all_to_all | solution.py:158
  585.2 163.5 %copy-start.6 = (pred[256]{0:T(512)(128)(4,1)S(1)}, pred[256]{0:T(512)(128)(4,1)}, u32[]{:S(2)}) copy-start(pred[256]{0:T(512)(128)(4,1)} %get-tuple-element.31) | copy-start | bytes 772
  585.9 5.4 copy-start.2
Sparse Core Ops, SparseCore 0:
  36.5 124.7 all-reduce.4
  164.5 69.2 all-reduce.6
  272.3 138.9 all-reduce.8
  414.9 67.8 reduce-scatter.3
  484.3 100.8 all-gather.1
